TPU v7x, 32 devices: a whole 2x2x4 slice. The times are simulated.
32 devices in a mesh: pipe: 2 (over x), dp: 4 (over z), mp: 4 (over y, core).
Axes of the slice: x: 2, y: 2, z: 4, core: 2. Of those that a mesh axis runs over, the one named last changes fastest.
Arguments:
- section_in: bfloat16 [2, 12, 729, 1152], P('pipe', 'dp'), may hold values from -6 to 6
- ln1_gain: bfloat16 [2, 1152], P('pipe'), may hold values from 0.099609375 to 1.8984375
- ln1_bias: bfloat16 [2, 1152], P('pipe'), may hold values from -3 to 3
- qkv_weight: bfloat16 [2, 1152, 3, 1152], P('pipe', None, None, 'mp'), may hold values from -0.1875 to 0.1875
- qv_bias: bfloat16 [2, 2, 1152], P('pipe', None, 'mp'), may hold values from -3 to 3
- out_weight: bfloat16 [2, 1152, 1152], P('pipe', 'mp'), may hold values from -3 to 3
- out_bias: bfloat16 [2, 1152], P('pipe'), may hold values from -3 to 3
- ln2_gain: bfloat16 [2, 1152], P('pipe'), may hold values from 0.099609375 to 1.8984375
- ln2_bias: bfloat16 [2, 1152], P('pipe'), may hold values from -3 to 3
- fc1_weight: bfloat16 [2, 1152, 4304], P('pipe', None, 'mp'), may hold values from -0.1875 to 0.1875
- fc1_bias: bfloat16 [2, 4304], P('pipe', 'mp'), may hold values from -3 to 3
- fc2_weight: bfloat16 [2, 4304, 1152], P('pipe', 'mp'), may hold values from -0.1875 to 0.1875
- fc2_bias: bfloat16 [2, 1152], P('pipe'), may hold values from -4 to 4
Outputs:
- section_out: bfloat16 [2, 12, 729, 1152], P('pipe', 'dp')
- grad_ln1_gain: float32 [2, 1152], P('pipe')
- grad_ln1_bias: float32 [2, 1152], P('pipe')
- grad_qkv_weight: float32 [2, 1152, 3, 1152], P('pipe', None, None, 'mp')
- grad_qv_bias: float32 [2, 2, 1152], P('pipe', None, 'mp')
- grad_out_weight: float32 [2, 1152, 1152], P('pipe', 'mp')
- grad_out_bias: float32 [2, 1152], P('pipe')
- grad_ln2_gain: float32 [2, 1152], P('pipe')
- grad_ln2_bias: float32 [2, 1152], P('pipe')
- grad_fc1_weight: float32 [2, 1152, 4304], P('pipe', None, 'mp')
- grad_fc1_bias: float32 [2, 4304], P('pipe', 'mp')
- grad_fc2_weight: float32 [2, 4304, 1152], P('pipe', 'mp')
- grad_fc2_bias: float32 [2, 1152], P('pipe')
All inputs are finite; a program needn't handle non-finite values.
Results may differ from a plain program's by a relative error of at most 0.028.
Values may be sent and summed in bfloat16 or wider, within the bound.
A program may use at most 320 MiB of HBM per device.

v0:
```python
import jax
import jax.numpy as jnp
from jax import lax
from jax.sharding import PartitionSpec as P

HDIM = 72
EPSILON = 1e-06
GELU_SCALE = 0.7978845608028654
GELU_CUBIC = 0.044715


def shifted(value, axis, by):
    peers = lax.axis_size(axis)
    pairs = [(i, i + by) for i in range(peers) if 0 <= i + by < peers]
    return lax.ppermute(value, axis, pairs)


def norm_rows(values, gain_vec, shift_vec):
    center = values - jnp.mean(values, axis=-1, keepdims=True)
    inv_std = lax.rsqrt(jnp.mean(center * center, axis=-1, keepdims=True) + EPSILON)
    x_hat = center * inv_std
    return (x_hat * gain_vec + shift_vec, x_hat, inv_std)


def norm_back(d_out, x_hat, inv_std, gain_vec):
    d_hat = d_out * gain_vec
    inner = (
        d_hat
        - jnp.mean(d_hat, axis=-1, keepdims=True)
        - x_hat * jnp.mean(d_hat * x_hat, axis=-1, keepdims=True)
    )
    return (inv_std * inner, jnp.sum(d_out * x_hat, axis=0), jnp.sum(d_out, axis=0))


def gelu_parts(pre_act):
    tanh_val = jnp.tanh(GELU_SCALE * (pre_act + GELU_CUBIC * pre_act * pre_act * pre_act))
    act_value = 0.5 * pre_act * (1.0 + tanh_val)
    act_slope = 0.5 * (1.0 + tanh_val) + 0.5 * pre_act * (
        1.0 - tanh_val * tanh_val
    ) * GELU_SCALE * (1.0 + 3.0 * GELU_CUBIC * pre_act * pre_act)
    return (act_value, act_slope)


def attend(query, key_rows, value_rows, scaling):
    scores = (
        jnp.einsum("qhd,khd->hqk", query, key_rows, preferred_element_type=jnp.float32) * scaling
    )
    row_max = jnp.max(scores, axis=-1, keepdims=True)
    exp_terms = jnp.exp(scores - row_max)
    row_total = jnp.sum(exp_terms, axis=-1, keepdims=True)
    attn_probs = (exp_terms / row_total).astype(jnp.bfloat16)
    mixed = jnp.einsum("hqk,khd->qhd", attn_probs, value_rows, preferred_element_type=jnp.float32)
    return (mixed, row_max + jnp.log(row_total))


def attend_back(query, key_rows, value_rows, log_total, d_mixed, scaling):
    scores = (
        jnp.einsum("qhd,khd->hqk", query, key_rows, preferred_element_type=jnp.float32) * scaling
    )
    attn_probs = jnp.exp(scores - log_total)
    probs_low = attn_probs.astype(jnp.bfloat16)
    d_values = jnp.einsum("hqk,qhd->khd", probs_low, d_mixed, preferred_element_type=jnp.float32)
    d_probs = jnp.einsum("qhd,khd->hqk", d_mixed, value_rows, preferred_element_type=jnp.float32)
    inner = jnp.sum(d_probs * attn_probs, axis=-1, keepdims=True)
    d_scores = (attn_probs * (d_probs - inner)).astype(jnp.bfloat16)
    d_query = (
        jnp.einsum("hqk,khd->qhd", d_scores, key_rows, preferred_element_type=jnp.float32) * scaling
    )
    d_keys = (
        jnp.einsum("hqk,qhd->khd", d_scores, query, preferred_element_type=jnp.float32) * scaling
    )
    return (
        d_query.astype(jnp.bfloat16),
        d_keys.astype(jnp.bfloat16),
        d_values.astype(jnp.bfloat16),
    )


def attention_part(residual, gain_one, shift_one, w_qkv, bias_qv, scaling):
    row_count = residual.shape[0]
    normed = norm_rows(residual, gain_one, shift_one)[0]
    packed = jnp.dot(
        normed.astype(jnp.bfloat16), w_qkv, preferred_element_type=jnp.float32
    ).reshape(row_count, 3, -1)
    bias_three = jnp.stack([bias_qv[0], jnp.zeros_like(bias_qv[0]), bias_qv[1]])
    packed = (packed + bias_three).astype(jnp.bfloat16)
    local_width = packed.shape[2]
    head_count = local_width // HDIM
    query = packed[:, 0].reshape(row_count, head_count, HDIM)
    key_rows = packed[:, 1].reshape(row_count, head_count, HDIM)
    value_rows = packed[:, 2].reshape(row_count, head_count, HDIM)
    mixed, log_total = attend(query, key_rows, value_rows, scaling)
    return (packed, log_total, mixed.reshape(row_count, local_width).astype(jnp.bfloat16))


def attention_back(packed, log_total, d_attn, mixed_low, w_out, scaling):
    row_count = packed.shape[0]
    local_width = packed.shape[2]
    head_count = local_width // HDIM
    grad_w_out = jnp.einsum("sc,sd->cd", mixed_low, d_attn, preferred_element_type=jnp.float32)
    d_mixed = jnp.einsum("sd,cd->sc", d_attn, w_out, preferred_element_type=jnp.float32).astype(
        jnp.bfloat16
    )
    query = packed[:, 0].reshape(row_count, head_count, HDIM)
    key_rows = packed[:, 1].reshape(row_count, head_count, HDIM)
    value_rows = packed[:, 2].reshape(row_count, head_count, HDIM)
    d_query, d_keys, d_values = attend_back(
        query,
        key_rows,
        value_rows,
        log_total,
        d_mixed.reshape(row_count, head_count, HDIM),
        scaling,
    )
    d_query = d_query.reshape(row_count, local_width)
    d_values = d_values.reshape(row_count, local_width)
    d_packed = jnp.stack(
        [d_query, d_keys.reshape(row_count, local_width), d_values], axis=1
    ).reshape(row_count, 3 * local_width)
    grad_bias_qv = jnp.stack(
        [
            jnp.sum(d_query.astype(jnp.float32), axis=0),
            jnp.sum(d_values.astype(jnp.float32), axis=0),
        ]
    )
    return (grad_w_out, d_packed, grad_bias_qv)


def layer_forward(inputs, weights, scaling):
    (
        gain_one,
        shift_one,
        w_qkv,
        bias_qv,
        w_out,
        bias_out,
        gain_two,
        shift_two,
        w_fc1,
        bias_fc1,
        w_fc2,
        bias_fc2,
    ) = weights
    residual = inputs.astype(jnp.float32)
    packed, log_total, mixed_low = attention_part(
        residual, gain_one, shift_one, w_qkv, bias_qv, scaling
    )
    branch = lax.psum(
        jnp.dot(mixed_low, w_out, preferred_element_type=jnp.float32).astype(jnp.bfloat16), "mp"
    ).astype(jnp.float32)
    mid_stream = residual + branch + bias_out
    normed_two = norm_rows(mid_stream, gain_two, shift_two)[0]
    pre_act = (
        jnp.dot(normed_two.astype(jnp.bfloat16), w_fc1, preferred_element_type=jnp.float32)
        + bias_fc1
    )
    act_out = gelu_parts(pre_act)[0]
    branch_two = lax.psum(
        jnp.dot(act_out.astype(jnp.bfloat16), w_fc2, preferred_element_type=jnp.float32).astype(
            jnp.bfloat16
        ),
        "mp",
    ).astype(jnp.float32)
    layer_out = (mid_stream + branch_two + bias_fc2).astype(jnp.bfloat16)
    kept_state = (inputs, packed, log_total, mixed_low, mid_stream)
    return (layer_out, kept_state)


def layer_backward(kept_state, d_out, weights, scaling):
    (
        gain_one,
        shift_one,
        w_qkv,
        bias_qv,
        w_out,
        bias_out,
        gain_two,
        shift_two,
        w_fc1,
        bias_fc1,
        w_fc2,
        bias_fc2,
    ) = weights
    inputs, packed, log_total, mixed_low, mid_stream = (
        kept_state[0],
        kept_state[1],
        kept_state[2],
        kept_state[3],
        kept_state[4],
    )
    residual = inputs.astype(jnp.float32)
    normed, hat_one, std_one = norm_rows(residual, gain_one, shift_one)
    normed_two, hat_two, std_two = norm_rows(mid_stream, gain_two, shift_two)
    normed_two_low = normed_two.astype(jnp.bfloat16)
    pre_act = jnp.dot(normed_two_low, w_fc1, preferred_element_type=jnp.float32) + bias_fc1
    act_out, act_slope = gelu_parts(pre_act)
    act_low = act_out.astype(jnp.bfloat16)
    grad_b_two = jnp.sum(d_out, axis=0)
    d_mlp = d_out.astype(jnp.bfloat16)
    grad_w_two = jnp.einsum("sf,sd->fd", act_low, d_mlp, preferred_element_type=jnp.float32)
    d_act = jnp.einsum("sd,fd->sf", d_mlp, w_fc2, preferred_element_type=jnp.float32)
    d_pre = (d_act * act_slope).astype(jnp.bfloat16)
    grad_w_one = jnp.einsum("sd,sf->df", normed_two_low, d_pre, preferred_element_type=jnp.float32)
    grad_b_one = jnp.sum(d_pre.astype(jnp.float32), axis=0)
    d_norm_two = lax.psum(
        jnp.einsum("sf,df->sd", d_pre, w_fc1, preferred_element_type=jnp.float32).astype(
            jnp.bfloat16
        ),
        "mp",
    ).astype(jnp.float32)
    d_mid_norm, grad_gain_two, grad_shift_two = norm_back(d_norm_two, hat_two, std_two, gain_two)
    d_mid = d_out + d_mid_norm
    grad_bias_out = jnp.sum(d_mid, axis=0)
    grad_w_out, d_packed, grad_bias_qv = attention_back(
        packed, log_total, d_mid.astype(jnp.bfloat16), mixed_low, w_out, scaling
    )
    grad_w_qkv = jnp.einsum(
        "sd,sc->dc", normed.astype(jnp.bfloat16), d_packed, preferred_element_type=jnp.float32
    )
    d_norm_one = lax.psum(
        jnp.einsum("sc,dc->sd", d_packed, w_qkv, preferred_element_type=jnp.float32).astype(
            jnp.bfloat16
        ),
        "mp",
    ).astype(jnp.float32)
    d_res_norm, grad_gain_one, grad_shift_one = norm_back(d_norm_one, hat_one, std_one, gain_one)
    d_input = (d_mid + d_res_norm).astype(jnp.bfloat16)
    grads = (
        grad_gain_one,
        grad_shift_one,
        grad_w_qkv,
        grad_bias_qv,
        grad_w_out,
        grad_bias_out,
        grad_gain_two,
        grad_shift_two,
        grad_w_one,
        grad_b_one,
        grad_w_two,
        grad_b_two,
    )
    return (d_input, grads)


def on_device(
    section_in,
    ln1_gain,
    ln1_bias,
    qkv_weight,
    qv_bias,
    out_weight,
    out_bias,
    ln2_gain,
    ln2_bias,
    fc1_weight,
    fc1_bias,
    fc2_weight,
    fc2_bias,
):
    section_pos = lax.axis_index("pipe")
    is_first = section_pos == 0
    feed_rows = section_in[0]
    micro_count = feed_rows.shape[0]
    model_width = feed_rows.shape[2]
    scaling = HDIM ** (-0.5)
    weights = (
        ln1_gain[0].astype(jnp.float32),
        ln1_bias[0].astype(jnp.float32),
        qkv_weight[0].reshape(model_width, -1),
        qv_bias[0].astype(jnp.float32),
        out_weight[0],
        out_bias[0].astype(jnp.float32),
        ln2_gain[0].astype(jnp.float32),
        ln2_bias[0].astype(jnp.float32),
        fc1_weight[0],
        fc1_bias[0].astype(jnp.float32),
        fc2_weight[0],
        fc2_bias[0].astype(jnp.float32),
    )

    def pick_side(low_side, high_side):
        return jnp.where(is_first, low_side, high_side)

    arriving = jnp.zeros(feed_rows.shape[1:], jnp.bfloat16)
    kept_ticks = []
    results = []
    for tick_num in range(micro_count + 1):
        pick_index = jnp.clip(tick_num - section_pos, 0, micro_count - 1)
        own_rows = lax.dynamic_index_in_dim(feed_rows, pick_index, 0, keepdims=False)
        layer_out, kept_state = layer_forward(
            jnp.where(is_first, own_rows, arriving), weights, scaling
        )
        kept_ticks.append(kept_state)
        results.append(layer_out)
        if tick_num < micro_count:
            arriving = shifted(layer_out, "pipe", 1)
    back_rows = jnp.zeros(feed_rows.shape[1:], jnp.bfloat16)
    totals = None
    sent_grads = []
    for tick_num in range(micro_count + 1):
        pick_index = jnp.clip(tick_num - 1 + section_pos, 0, micro_count - 1)
        own_rows = lax.dynamic_index_in_dim(feed_rows, pick_index, 0, keepdims=False)
        d_out = jnp.where(is_first, back_rows, own_rows).astype(jnp.float32)
        kept_state = jax.tree.map(
            pick_side, kept_ticks[max(tick_num - 1, 0)], kept_ticks[min(tick_num + 1, micro_count)]
        )
        d_input, grads = layer_backward(kept_state, d_out, weights, scaling)
        is_live = jnp.where(is_first, tick_num >= 1, tick_num < micro_count)
        grads = tuple((jnp.where(is_live, grad_item, 0.0) for grad_item in grads))
        totals = (
            grads
            if totals is None
            else tuple((left_item + right_item for left_item, right_item in zip(totals, grads)))
        )
        sent_grads.append(d_input)
        if tick_num < micro_count:
            back_rows = shifted(d_input, "pipe", -1)
    share_list = (
        lax.psum_scatter(
            totals[2].astype(jnp.bfloat16), "dp", scatter_dimension=0, tiled=True
        ).astype(jnp.float32),
        lax.psum_scatter(
            totals[4].astype(jnp.bfloat16), "dp", scatter_dimension=1, tiled=True
        ).astype(jnp.float32),
        lax.psum_scatter(
            totals[8].astype(jnp.bfloat16), "dp", scatter_dimension=0, tiled=True
        ).astype(jnp.float32),
        lax.psum_scatter(
            totals[10].astype(jnp.bfloat16), "dp", scatter_dimension=1, tiled=True
        ).astype(jnp.float32),
    )
    whole = (
        lax.all_gather(share_list[0].astype(jnp.bfloat16), "dp", axis=0, tiled=True).astype(
            jnp.float32
        ),
        lax.all_gather(share_list[1].astype(jnp.bfloat16), "dp", axis=1, tiled=True).astype(
            jnp.float32
        ),
        lax.all_gather(share_list[2].astype(jnp.bfloat16), "dp", axis=0, tiled=True).astype(
            jnp.float32
        ),
        lax.all_gather(share_list[3].astype(jnp.bfloat16), "dp", axis=1, tiled=True).astype(
            jnp.float32
        ),
    )
    small = lax.psum(
        (totals[0], totals[1], totals[3], totals[5], totals[6], totals[7], totals[9], totals[11]),
        "dp",
    )
    forward_rows = jnp.stack(results[1:])
    backward_rows = jnp.stack(sent_grads[1:])
    section_out = jnp.where(is_first, backward_rows, forward_rows)[None]
    return (
        section_out,
        small[0][None],
        small[1][None],
        whole[0].reshape(model_width, 3, -1)[None],
        small[2][None],
        whole[1][None],
        small[3][None],
        small[4][None],
        small[5][None],
        whole[2][None],
        small[6][None],
        whole[3][None],
        small[7][None],
    )


def solution(mesh):
    placed = (
        P("pipe", "dp", None, None),
        P("pipe", None),
        P("pipe", None),
        P("pipe", None, None, "mp"),
        P("pipe", None, "mp"),
        P("pipe", "mp", None),
        P("pipe", None),
        P("pipe", None),
        P("pipe", None),
        P("pipe", None, "mp"),
        P("pipe", "mp"),
        P("pipe", "mp", None),
        P("pipe", None),
    )
    return jax.shard_map(
        on_device,
        mesh=mesh,
        in_specs=placed,
        out_specs=(
            P("pipe", "dp", None, None),
            P("pipe", None),
            P("pipe", None),
            P("pipe", None, None, "mp"),
            P("pipe", None, "mp"),
            P("pipe", "mp", None),
            P("pipe", None),
            P("pipe", None),
            P("pipe", None),
            P("pipe", None, "mp"),
            P("pipe", "mp"),
            P("pipe", "mp", None),
            P("pipe", None),
        ),
        check_vma=False,
    )
```

profile of v0, /device:TPU:0, one launch (start us, length us, event | category | flops | bytes accessed | tf_op | source)
XLA Modules:
  0.0 1629.2 jit_solution(3938570287198335092)
XLA Ops:
  27.6 47.4 %all-reduce.18.cloned.1.call-done = bf16[729,1152]{1,0:T(8,128)(2,1)} async-done(((bf16[729,1152]{1,0:T(8,128)(2,1)}), bf16[729,1152]{1,0:T(8,128)(2,1)}) %all-reduce.18.cloned.1.call-update) | async-done | bytes 1679632 | tf_op jit(solution)/shard_map/psum | solution.py:148
  80.3 13.7 convolution_convert_fusion.15
  94.1 45.0 %all-reduce.20.cloned.1.call-done = bf16[729,1152]{1,0:T(8,128)(2,1)} async-done(((bf16[729,1152]{1,0:T(8,128)(2,1)}), bf16[729,1152]{1,0:T(8,128)(2,1)}) %all-reduce.20.cloned.1.call-update) | async-done | bytes 1679632 | tf_op jit(solution)/shard_map/psum | solution.py:158
  139.1 4.6 add_convert_fusion.10
  143.7 5.0 collective-permute-start
  148.7 34.8 %collective-permute-done = bf16[729,1152]{1,0:T(8,128)(2,1)} collective-permute-done((bf16[729,1152]{1,0:T(8,128)(2,1)}, bf16[729,1152]{1,0:T(8,128)(2,1)}, u32[]{:S(2)}, u32[]{:S(2)}) %collective-permute-start) | collective-permute-done | bytes 1679648 | tf_op jit(solution)/shard_map/ppermute | solution.py:15
  202.0 46.4 %all-reduce.22.cloned.1.call-done = bf16[729,1152]{1,0:T(8,128)(2,1)} async-done(((bf16[729,1152]{1,0:T(8,128)(2,1)}), bf16[729,1152]{1,0:T(8,128)(2,1)}) %all-reduce.22.cloned.1.call-update) | async-done | bytes 1679632 | tf_op jit(solution)/shard_map/psum | solution.py:148
  258.2 7.0 convert_reduce_fusion.23
  270.2 13.9 convolution_convert_fusion.12
  284.2 72.7 %all-reduce.38.cloned.1.call-done = (bf16[729,1152]{1,0:T(8,128)(2,1)}, bf16[729,1152]{1,0:T(8,128)(2,1)}) async-done(((bf16[729,1152]{1,0:T(8,128)(2,1)}, bf16[729,1152]{1,0:T(8,128)(2,1)}), (bf16[729,1152]{1,0:T(8,128)(2,1)}, bf16[729,1152]{1,0:T(8,128)(2,1)})) %all-reduce.38.cloned.1.call-update) | async-done | bytes 3359248 | tf_op jit(solution)/shard_map/psum | solution.py:205
  369.8 30.1 %collective-permute-done.2 = bf16[729,1152]{1,0:T(8,128)(2,1)S(1)} collective-permute-done((bf16[729,1152]{1,0:T(8,128)(2,1)S(1)}, bf16[729,1152]{1,0:T(8,128)(2,1)S(1)}, u32[]{:S(2)}, u32[]{:S(2)}) %collective-permute-start.2) | collective-permute-done | bytes 1679648 | tf_op jit(solution)/shard_map/ppermute | solution.py:15
  399.9 4.5 convert_reduce_fusion.16
  408.2 4.8 multiply_reduce_fusion.3
  413.0 10.2 multiply_convert_fusion.3
  447.0 71.8 %all-reduce.36.cloned.1.call-done = (bf16[729,1152]{1,0:T(8,128)(2,1)}, bf16[729,1152]{1,0:T(8,128)(2,1)}) async-done(((bf16[729,1152]{1,0:T(8,128)(2,1)}, bf16[729,1152]{1,0:T(8,128)(2,1)}), (bf16[729,1152]{1,0:T(8,128)(2,1)}, bf16[729,1152]{1,0:T(8,128)(2,1)})) %all-reduce.36.cloned.1.call-update) | async-done | bytes 3359248 | tf_op jit(solution)/shard_map/psum | solution.py:220
  530.8 36.7 %collective-permute-done.1 = bf16[729,1152]{1,0:T(8,128)(2,1)} collective-permute-done((bf16[729,1152]{1,0:T(8,128)(2,1)}, bf16[729,1152]{1,0:T(8,128)(2,1)}, u32[]{:S(2)}, u32[]{:S(2)}) %collective-permute-start.1) | collective-permute-done | bytes 1679648 | tf_op jit(solution)/shard_map/ppermute | solution.py:15
  567.5 6.9 fusion.440
  576.6 13.7 convolution_convert_fusion.9
  590.4 4.6 convolution_add_fusion.5
  595.0 6.1 convert_reduce_fusion.22
  606.2 71.9 %all-reduce.34.cloned.1.call-done = (bf16[729,1152]{1,0:T(8,128)(2,1)}, bf16[729,1152]{1,0:T(8,128)(2,1)}) async-done(((bf16[729,1152]{1,0:T(8,128)(2,1)}, bf16[729,1152]{1,0:T(8,128)(2,1)}), (bf16[729,1152]{1,0:T(8,128)(2,1)}, bf16[729,1152]{1,0:T(8,128)(2,1)})) %all-reduce.34.cloned.1.call-update) | async-done | bytes 3359248 | tf_op jit(solution)/shard_map/psum | solution.py:205
  691.5 29.9 %collective-permute-done.4 = bf16[729,1152]{1,0:T(8,128)(2,1)S(1)} collective-permute-done((bf16[729,1152]{1,0:T(8,128)(2,1)S(1)}, bf16[729,1152]{1,0:T(8,128)(2,1)S(1)}, u32[]{:S(2)}, u32[]{:S(2)}) %collective-permute-start.4) | collective-permute-done | bytes 1679648 | tf_op jit(solution)/shard_map/ppermute | solution.py:15
  727.3 4.4 broadcast_select_fusion.6
  742.7 4.9 multiply_reduce_fusion.2
  747.6 10.2 multiply_convert_fusion.2
  763.4 6.7 broadcast_select_fusion.11
  783.3 4.9 fusion.452
  788.2 62.6 %all-reduce.32.cloned.1.call-done = (bf16[729,1152]{1,0:T(8,128)(2,1)}, bf16[729,1152]{1,0:T(8,128)(2,1)}) async-done(((bf16[729,1152]{1,0:T(8,128)(2,1)}, bf16[729,1152]{1,0:T(8,128)(2,1)}), (bf16[729,1152]{1,0:T(8,128)(2,1)}, bf16[729,1152]{1,0:T(8,128)(2,1)})) %all-reduce.32.cloned.1.call-update) | async-done | bytes 3359248 | tf_op jit(solution)/shard_map/psum | solution.py:220
  866.2 32.5 %collective-permute-done.3 = bf16[729,1152]{1,0:T(8,128)(2,1)S(1)} collective-permute-done((bf16[729,1152]{1,0:T(8,128)(2,1)S(1)}, bf16[729,1152]{1,0:T(8,128)(2,1)S(1)}, u32[]{:S(2)}, u32[]{:S(2)}) %collective-permute-start.3) | collective-permute-done | bytes 1679648 | tf_op jit(solution)/shard_map/ppermute | solution.py:15
  901.4 5.6 convert_reduce_fusion.21
  912.4 6.2 fusion.453
  922.9 33.5 %all-reduce.24.cloned.1.call-done = bf16[729,1152]{1,0:T(8,128)(2,1)} async-done(((bf16[729,1152]{1,0:T(8,128)(2,1)}), bf16[729,1152]{1,0:T(8,128)(2,1)}) %all-reduce.24.cloned.1.call-update) | async-done | bytes 1679632 | tf_op jit(solution)/shard_map/psum | solution.py:205
  956.4 4.7 fusion.151
  967.1 6.6 convert_reduce_fusion.26
  973.8 4.7 multiply_reduce_fusion.1
  978.5 10.2 multiply_convert_fusion.1
  1000.7 42.8 %all-reduce.26.cloned.1.call-done = bf16[729,1152]{1,0:T(8,128)(2,1)} async-done(((bf16[729,1152]{1,0:T(8,128)(2,1)}), bf16[729,1152]{1,0:T(8,128)(2,1)}) %all-reduce.26.cloned.1.call-update) | async-done | bytes 1679632 | tf_op jit(solution)/shard_map/psum | solution.py:220
  1056.3 34.5 %collective-permute-done.5 = bf16[729,1152]{1,0:T(8,128)(2,1)S(1)} collective-permute-done((bf16[729,1152]{1,0:T(8,128)(2,1)S(1)}, bf16[729,1152]{1,0:T(8,128)(2,1)S(1)}, u32[]{:S(2)}, u32[]{:S(2)}) %collective-permute-start.5) | collective-permute-done | bytes 1679648 | tf_op jit(solution)/shard_map/ppermute | solution.py:15
  1092.9 5.0 convert_reduce_fusion.20
  1105.4 6.2 fusion.235
  1111.6 35.5 %all-reduce.28.cloned.1.call-done = bf16[729,1152]{1,0:T(8,128)(2,1)} async-done(((bf16[729,1152]{1,0:T(8,128)(2,1)}), bf16[729,1152]{1,0:T(8,128)(2,1)}) %all-reduce.28.cloned.1.call-update) | async-done | bytes 1679632 | tf_op jit(solution)/shard_map/psum | solution.py:205
  1156.7 5.4 convert_reduce_fusion.24
  1162.2 4.8 multiply_reduce_fusion
  1167.0 10.2 multiply_convert_fusion
  1192.2 5.3 convolution_select_fusion.1
  1202.9 6.5 fusion.5
  1209.7 7.9 fusion.432
  1224.7 13.9 convolution_convert_fusion.4
  1238.6 7.9 fusion.433
  1250.7 8.8 fusion.1
  1259.5 4.6 fusion.6
  1265.0 24.7 %reduce-scatter.11.cloned.1.call-done = bf16[1076,288]{0,1:T(8,128)(2,1)} async-done(((bf16[1076,1152]{0,1:T(8,128)(2,1)}), bf16[1076,288]{0,1:T(8,128)(2,1)}) %reduce-scatter.11.cloned.1.call-update) | async-done | bytes 619792 | tf_op jit(solution)/shard_map/reduce_scatter | solution.py:328
  1290.8 25.6 %reduce-scatter.15.cloned.1.call-done = bf16[288,288]{1,0:T(8,128)(2,1)} async-done(((bf16[1152,288]{1,0:T(8,128)(2,1)}), bf16[288,288]{1,0:T(8,128)(2,1)}) %reduce-scatter.15.cloned.1.call-update) | async-done | bytes 165904
  1316.4 18.8 %all_gather.13 = bf16[288,1152]{0,1:T(8,128)(2,1)S(1)} all-gather(bf16[288,288]{0,1:T(8,128)(2,1)} %bitcast.466), channel_id=1, replica_groups=mesh['pipe'=2,'dp'=4,'mp'=4] {'dp'}, dimensions={1}, use_global_device_ids=true | all-gather | bytes 829440 | tf_op jit(solution)/shard_map/all_gather | solution.py:336
  1339.7 51.4 %all-reduce.30.cloned.1.call-done = (bf16[729,1152]{1,0:T(8,128)(2,1)}, bf16[729,1152]{1,0:T(8,128)(2,1)}) async-done(((bf16[729,1152]{1,0:T(8,128)(2,1)}, bf16[729,1152]{1,0:T(8,128)(2,1)}), (bf16[729,1152]{1,0:T(8,128)(2,1)}, bf16[729,1152]{1,0:T(8,128)(2,1)})) %all-reduce.30.cloned.1.call-update) | async-done | bytes 3359248 | tf_op jit(solution)/shard_map/psum | solution.py:220
  1394.7 22.3 %all-reduce = (f32[1,1152]{1,0:T(1,128)}, f32[1,1152]{1,0:T(1,128)}, f32[1,2,288]{2,1,0:T(2,128)}, f32[1,1152]{1,0:T(1,128)}, f32[1,1152]{1,0:T(1,128)}, /*index...) all-reduce(f32[1,1152]{1,0:T(1,128)S(1)} %broadcast_in_dim.101, ...), channel_id=1, replica_groups=mesh['pipe'=2,'dp'=4,'mp'=4] {'dp'}, use_global_device_ids=true, to_apply=%region_80.81 | all-reduce | flops 8564 | bytes 68512 | tf_op jit(solution)/shard_map/psum | solution.py:346
  1417.0 4.5 fusion.231
  1421.5 26.0 %reduce-scatter.9.cloned.1.call-done = bf16[288,1076]{1,0:T(8,128)(2,1)} async-done(((bf16[1152,1076]{1,0:T(8,128)(2,1)}), bf16[288,1076]{1,0:T(8,128)(2,1)}) %reduce-scatter.9.cloned.1.call-update) | async-done | bytes 619792 | tf_op jit(solution)/shard_map/reduce_scatter | solution.py:325
  1456.2 37.6 %all-gather.4.cloned.1.call-done = bf16[1152,864]{1,0:T(8,128)(2,1)} async-done(((bf16[288,864]{1,0:T(8,128)(2,1)}), bf16[1152,864]{1,0:T(8,128)(2,1)}) %all-gather.4.cloned.1.call-update) | async-done | bytes 1990672 | tf_op jit(solution)/shard_map/all_gather | solution.py:333
  1501.6 47.7 %all-gather.8.cloned.1.call-done = bf16[1076,1152]{0,1:T(8,128)(2,1)} async-done(((bf16[1076,288]{0,1:T(8,128)(2,1)}), bf16[1076,1152]{0,1:T(8,128)(2,1)}) %all-gather.8.cloned.1.call-update) | async-done | bytes 2479120 | tf_op jit(solution)/shard_map/all_gather | solution.py:342
  1549.4 4.4 bitcast_convert_fusion
  1553.8 12.8 copy.131
  1566.5 38.3 %all-gather.6.cloned.1.call-done = bf16[1152,1076]{1,0:T(8,128)(2,1)} async-done(((bf16[288,1076]{1,0:T(8,128)(2,1)}), bf16[1152,1076]{1,0:T(8,128)(2,1)}) %all-gather.6.cloned.1.call-update) | async-done | bytes 2479120 | tf_op jit(solution)/shard_map/all_gather | solution.py:339
  1609.3 12.7 copy.130
  (616 shorter events, 306.1 us)
Async XLA Ops:
  7.2 73.1 %copy-start = (bf16[1,1152,1076]{1,2,0:T(8,128)(2,1)S(1)}, bf16[1,1152,1076]{1,2,0:T(8,128)(2,1)}, u32[]{:S(2)}) copy-start(bf16[1,1152,1076]{1,2,0:T(8,128)(2,1)} %param.22) | copy-start | bytes 7437316
  7.2 67.8 %all-reduce.18.cloned.1.call-start = ((), (), s32[]{:S(2)}) async-start(), calls=%async_computation.4 | async-start | bytes 3391488 | tf_op jit(solution)/shard_map/psum | solution.py:148
  27.2 111.9 %all-reduce.20.cloned.1.call-start = ((), (), s32[]{:S(2)}) async-start(), calls=%async_computation.5 | async-start | bytes 3391488 | tf_op jit(solution)/shard_map/psum | solution.py:158
  94.0 154.4 %all-reduce.22.cloned.1.call-start = ((), (), s32[]{:S(2)}) async-start(), calls=%async_computation.6 | async-start | bytes 3391488 | tf_op jit(solution)/shard_map/psum | solution.py:148
  94.1 584.1 %copy-start.108 = (f32[1152]{0:T(1024)}, f32[1152]{0:T(1024)S(1)}, u32[]{:S(2)}) copy-start(f32[1152]{0:T(1024)S(1)} %convert_reduce_fusion.32) | copy-start | bytes 13828
  143.7 39.8 %collective-permute-start = (bf16[729,1152]{1,0:T(8,128)(2,1)}, bf16[729,1152]{1,0:T(8,128)(2,1)}, u32[]{:S(2)}, u32[]{:S(2)}) collective-permute-start(bf16[729,1152]{1,0:T(8,128)(2,1)} %add_convert_fusion.10), channel_id=1, source_target_pairs={{0,16},{1,17},{2,18},{3,19},{4,20},{5,21},{6,22},{7,23},{8,24},{9,... | collective-permute-start | bytes 5038856 | tf_op jit(solution)/shard_map/ppermute | solution.py:15
  201.7 155.2 %all-reduce.38.cloned.1.call-start = ((), (), s32[]{:S(2)}) async-start(), calls=%async_computation.21 | async-start | bytes 6782976 | tf_op jit(solution)/shard_map/psum | solution.py:205
  255.0 144.8 %copy-start.110 = (f32[729]{0:T(1024)}, f32[729]{0:T(1024)S(1)}, u32[]{:S(2)}) copy-start(f32[729]{0:T(1024)S(1)} %broadcast_multiply_fusion.28) | copy-start | bytes 8752
  255.5 144.3 %copy-start.116 = (f32[729]{0:T(1024)}, f32[729]{0:T(1024)S(1)}, u32[]{:S(2)}) copy-start(f32[729]{0:T(1024)S(1)} %add_rsqrt_fusion.12) | copy-start | bytes 8752
  284.2 234.6 %all-reduce.36.cloned.1.call-start = ((), (), s32[]{:S(2)}) async-start(), calls=%async_computation.20 | async-start | bytes 6782976 | tf_op jit(solution)/shard_map/psum | solution.py:220
  360.4 39.5 %collective-permute-start.2 = (bf16[729,1152]{1,0:T(8,128)(2,1)S(1)}, bf16[729,1152]{1,0:T(8,128)(2,1)S(1)}, u32[]{:S(2)}, u32[]{:S(2)}) collective-permute-start(bf16[729,1152]{1,0:T(8,128)(2,1)S(1)} %add_convert_fusion.7), channel_id=1, source_target_pairs={{0,16},{1,17},{2,18},{3,19},{4,20},{5,21},{6,22},{7,23},{8,24},{9,... | collective-permute-start | bytes 5038856 | tf_op jit(solution)/shard_map/ppermute | solution.py:15
  364.4 35.4 %slice-start = ((s8[5087232]{0:T(1024)(128)(4,1)}), s8[4194304]{0:T(1024)(128)(4,1)S(1)}, s32[]{:S(2)}) async-start(s8[5087232]{0:T(1024)(128)(4,1)} %bitcast.390), calls=%async_computation.22 | async-start | bytes 8388608
  364.5 35.4 %slice-start.1 = ((s8[5087232]{0:T(1024)(128)(4,1)}), s8[892928]{0:T(1024)(128)(4,1)S(1)}, s32[]{:S(2)}) async-start(s8[5087232]{0:T(1024)(128)(4,1)} %bitcast.390), calls=%async_computation.23 | async-start | bytes 1785856
  365.9 42.3 %copy-start.1 = (f32[4,729,729]{1,2,0:T(8,128)}, f32[4,729,729]{1,2,0:T(8,128)S(1)}, u32[]{:S(2)}) copy-start(f32[4,729,729]{1,2,0:T(8,128)S(1)} %fusion.450) | copy-start | bytes 25509172
  444.8 233.3 %all-reduce.34.cloned.1.call-start = ((), (), s32[]{:S(2)}) async-start(), calls=%async_computation.19 | async-start | bytes 6782976 | tf_op jit(solution)/shard_map/psum | solution.py:205
  444.9 81.9 %copy-start.114 = (f32[729]{0:T(1024)}, f32[729]{0:T(1024)S(1)}, u32[]{:S(2)}) copy-start(f32[729]{0:T(1024)S(1)} %broadcast_multiply_fusion.25) | copy-start | bytes 8752
  446.9 79.8 %copy-start.120 = (f32[729]{0:T(1024)}, f32[729]{0:T(1024)S(1)}, u32[]{:S(2)}) copy-start(f32[729]{0:T(1024)S(1)} %add_rsqrt_fusion.11) | copy-start | bytes 8752
  526.7 40.8 %collective-permute-start.1 = (bf16[729,1152]{1,0:T(8,128)(2,1)}, bf16[729,1152]{1,0:T(8,128)(2,1)}, u32[]{:S(2)}, u32[]{:S(2)}) collective-permute-start(bf16[729,1152]{1,0:T(8,128)(2,1)} %fusion.121), channel_id=1, source_target_pairs={{16,0},{17,1},{18,2},{19,3},{20,4},{21,5},{22,6},{23,7},{24,8},{25... | collective-permute-start | bytes 5038856 | tf_op jit(solution)/shard_map/ppermute | solution.py:15
  528.0 39.5 %copy-start.4 = (bf16[729,1152]{1,0:T(8,128)(2,1)S(1)}, bf16[729,1152]{1,0:T(8,128)(2,1)}, u32[]{:S(2)}) copy-start(bf16[729,1152]{1,0:T(8,128)(2,1)} %get-tuple-element.155) | copy-start | bytes 5038852
  528.1 39.5 %copy-start.39 = (bf16[729,1152]{1,0:T(8,128)(2,1)S(1)}, bf16[729,1152]{1,0:T(8,128)(2,1)}, u32[]{:S(2)}) copy-start(bf16[729,1152]{1,0:T(8,128)(2,1)} %all-reduce.18.cloned.1.call-done) | copy-start | bytes 5038852
  574.4 113.1 %copy-start.112 = (f32[729]{0:T(1024)}, f32[729]{0:T(1024)S(1)}, u32[]{:S(2)}) copy-start(f32[729]{0:T(1024)S(1)} %broadcast_multiply_fusion.20) | copy-start | bytes 8752
  576.6 110.9 %copy-start.118 = (f32[729]{0:T(1024)}, f32[729]{0:T(1024)S(1)}, u32[]{:S(2)}) copy-start(f32[729]{0:T(1024)S(1)} %add_rsqrt_fusion.8) | copy-start | bytes 8752
  606.2 244.7 %all-reduce.32.cloned.1.call-start = ((), (), s32[]{:S(2)}) async-start(), calls=%async_computation.18 | async-start | bytes 6782976 | tf_op jit(solution)/shard_map/psum | solution.py:220
  681.7 39.7 %collective-permute-start.4 = (bf16[729,1152]{1,0:T(8,128)(2,1)S(1)}, bf16[729,1152]{1,0:T(8,128)(2,1)S(1)}, u32[]{:S(2)}, u32[]{:S(2)}) collective-permute-start(bf16[729,1152]{1,0:T(8,128)(2,1)S(1)} %add_convert_fusion.4), channel_id=1, source_target_pairs={{0,16},{1,17},{2,18},{3,19},{4,20},{5,21},{6,22},{7,23},{8,24},{9,... | collective-permute-start | bytes 5038856 | tf_op jit(solution)/shard_map/ppermute | solution.py:15
  689.8 31.6 %copy-start.5 = (bf16[729,1152]{1,0:T(8,128)(2,1)S(1)}, bf16[729,1152]{1,0:T(8,128)(2,1)}, u32[]{:S(2)}) copy-start(bf16[729,1152]{1,0:T(8,128)(2,1)} %get-tuple-element.155) | copy-start | bytes 5038852
  777.0 179.5 %all-reduce.24.cloned.1.call-start = ((), (), s32[]{:S(2)}) async-start(), calls=%async_computation.7 | async-start | bytes 3391488 | tf_op jit(solution)/shard_map/psum | solution.py:205
  858.2 40.6 %collective-permute-start.3 = (bf16[729,1152]{1,0:T(8,128)(2,1)S(1)}, bf16[729,1152]{1,0:T(8,128)(2,1)S(1)}, u32[]{:S(2)}, u32[]{:S(2)}) collective-permute-start(bf16[729,1152]{1,0:T(8,128)(2,1)S(1)} %fusion.114), channel_id=1, source_target_pairs={{16,0},{17,1},{18,2},{19,3},{20,4},{21,5},{22,6},{23,7},{24,8},{25... | collective-permute-start | bytes 5038856 | tf_op jit(solution)/shard_map/ppermute | solution.py:15
  866.2 40.8 %copy-start.172 = (f32[729,1076]{0,1:T(8,128)}, f32[729,1076]{0,1:T(8,128)S(1)}, u32[]{:S(2)}) copy-start(f32[729,1076]{0,1:T(8,128)S(1)} %convolution_add_fusion.3) | copy-start | bytes 9412852
  866.2 35.1 %copy-start.153 = (bf16[1,1076,1152]{2,1,0:T(8,128)(2,1)S(1)}, bf16[1,1076,1152]{2,1,0:T(8,128)(2,1)}, u32[]{:S(2)}) copy-start(bf16[1,1076,1152]{2,1,0:T(8,128)(2,1)} %param.24) | copy-start | bytes 7437316
  912.1 131.3 %all-reduce.26.cloned.1.call-start = ((), (), s32[]{:S(2)}) async-start(), calls=%async_computation.8 | async-start | bytes 3391488 | tf_op jit(solution)/shard_map/psum | solution.py:220
  998.3 148.8 %all-reduce.28.cloned.1.call-start = ((), (), s32[]{:S(2)}) async-start(), calls=%async_computation.9 | async-start | bytes 3391488 | tf_op jit(solution)/shard_map/psum | solution.py:205
  1050.2 40.7 %collective-permute-start.5 = (bf16[729,1152]{1,0:T(8,128)(2,1)S(1)}, bf16[729,1152]{1,0:T(8,128)(2,1)S(1)}, u32[]{:S(2)}, u32[]{:S(2)}) collective-permute-start(bf16[729,1152]{1,0:T(8,128)(2,1)S(1)} %fusion.107), channel_id=1, source_target_pairs={{16,0},{17,1},{18,2},{19,3},{20,4},{21,5},{22,6},{23,7},{24,8},{25... | collective-permute-start | bytes 5038856 | tf_op jit(solution)/shard_map/ppermute | solution.py:15
  1056.3 41.6 %copy-start.175 = (f32[729,1076]{0,1:T(8,128)}, f32[729,1076]{0,1:T(8,128)S(1)}, u32[]{:S(2)}) copy-start(f32[729,1076]{0,1:T(8,128)S(1)} %convolution_add_fusion.2) | copy-start | bytes 9412852
  1056.3 36.6 %copy-start.154 = (bf16[1,1076,1152]{2,1,0:T(8,128)(2,1)S(1)}, bf16[1,1076,1152]{2,1,0:T(8,128)(2,1)}, u32[]{:S(2)}) copy-start(bf16[1,1076,1152]{2,1,0:T(8,128)(2,1)} %param.24) | copy-start | bytes 7437316
  1102.9 161.5 %reduce-scatter.13.cloned.1.call-start = ((), (), s32[]{:S(2)}) async-start(), calls=%async_computation.15 | async-start | bytes 2580480 | tf_op jit(solution)/shard_map/reduce_scatter | solution.py:319
  1191.7 98.0 %reduce-scatter.11.cloned.1.call-start = ((), (), s32[]{:S(2)}) async-start(), calls=%async_computation.13 | async-start | bytes 3317760 | tf_op jit(solution)/shard_map/reduce_scatter | solution.py:328
  1209.4 106.9 %reduce-scatter.15.cloned.1.call-start = ((), (), s32[]{:S(2)}) async-start(), calls=%async_computation.16 | async-start | bytes 1105920
  1224.7 166.3 %all-reduce.30.cloned.1.call-start = ((), (), s32[]{:S(2)}) async-start(), calls=%async_computation.17 | async-start | bytes 6782976 | tf_op jit(solution)/shard_map/psum | solution.py:220
  1250.0 197.4 %reduce-scatter.9.cloned.1.call-start = ((), (), s32[]{:S(2)}) async-start(), calls=%async_computation.11 | async-start | bytes 3317760 | tf_op jit(solution)/shard_map/reduce_scatter | solution.py:325
  1264.2 25.9 %copy-start.141 = (f32[4,72]{1,0:T(4,128)S(1)}, f32[4,72]{1,0:T(4,128)}, u32[]{:S(2)}) copy-start(f32[4,72]{1,0:T(4,128)} %get-tuple-element.238) | copy-start | bytes 3460
  1264.2 26.0 %copy-start.142 = (f32[4,72]{1,0:T(4,128)S(1)}, f32[4,72]{1,0:T(4,128)}, u32[]{:S(2)}) copy-start(f32[4,72]{1,0:T(4,128)} %get-tuple-element.232) | copy-start | bytes 3460
  1264.2 26.1 %copy-start.122 = (f32[1152]{0:T(1024)S(1)}, f32[1152]{0:T(1024)}, u32[]{:S(2)}) copy-start(f32[1152]{0:T(1024)} %get-tuple-element.86) | copy-start | bytes 13828
  1264.2 26.1 %copy-start.124 = (f32[1152]{0:T(1024)S(1)}, f32[1152]{0:T(1024)}, u32[]{:S(2)}) copy-start(f32[1152]{0:T(1024)} %get-tuple-element.163) | copy-start | bytes 13828
  1264.2 26.1 %copy-start.126 = (f32[1152]{0:T(1024)S(1)}, f32[1152]{0:T(1024)}, u32[]{:S(2)}) copy-start(f32[1152]{0:T(1024)} %get-tuple-element.132) | copy-start | bytes 13828
  1264.2 26.2 %copy-start.143 = (f32[1076]{0:T(1024)S(1)}, f32[1076]{0:T(1024)}, u32[]{:S(2)}) copy-start(f32[1076]{0:T(1024)} %get-tuple-element.250) | copy-start | bytes 12916
  1264.2 26.2 %copy-start.144 = (f32[1076]{0:T(1024)S(1)}, f32[1076]{0:T(1024)}, u32[]{:S(2)}) copy-start(f32[1076]{0:T(1024)} %get-tuple-element.248) | copy-start | bytes 12916
  1264.2 26.2 %copy-start.145 = (f32[1076]{0:T(1024)S(1)}, f32[1076]{0:T(1024)}, u32[]{:S(2)}) copy-start(f32[1076]{0:T(1024)} %get-tuple-element.246) | copy-start | bytes 12916
  1264.2 26.2 %copy-start.128 = (f32[1152]{0:T(1024)S(1)}, f32[1152]{0:T(1024)}, u32[]{:S(2)}) copy-start(f32[1152]{0:T(1024)} %get-tuple-element.78) | copy-start | bytes 13828
  1264.2 26.2 %copy-start.129 = (f32[1152]{0:T(1024)S(1)}, f32[1152]{0:T(1024)}, u32[]{:S(2)}) copy-start(f32[1152]{0:T(1024)} %get-tuple-element.104) | copy-start | bytes 13828
  1264.2 26.2 %copy-start.132 = (f32[1152]{0:T(1024)S(1)}, f32[1152]{0:T(1024)}, u32[]{:S(2)}) copy-start(f32[1152]{0:T(1024)} %get-tuple-element.80) | copy-start | bytes 13828
  1264.3 26.2 %copy-start.133 = (f32[1152]{0:T(1024)S(1)}, f32[1152]{0:T(1024)}, u32[]{:S(2)}) copy-start(f32[1152]{0:T(1024)} %get-tuple-element.105) | copy-start | bytes 13828
  1264.3 26.2 %copy-start.136 = (f32[1152]{0:T(1024)S(1)}, f32[1152]{0:T(1024)}, u32[]{:S(2)}) copy-start(f32[1152]{0:T(1024)} %get-tuple-element.82) | copy-start | bytes 13828
  1264.3 26.2 %copy-start.137 = (f32[1152]{0:T(1024)S(1)}, f32[1152]{0:T(1024)}, u32[]{:S(2)}) copy-start(f32[1152]{0:T(1024)} %get-tuple-element.106) | copy-start | bytes 13828
  1264.3 26.2 %copy-start.123 = (f32[1152]{0:T(1024)S(1)}, f32[1152]{0:T(1024)}, u32[]{:S(2)}) copy-start(f32[1152]{0:T(1024)} %get-tuple-element.165) | copy-start | bytes 13828
  1264.3 26.2 %copy-start.125 = (f32[1152]{0:T(1024)S(1)}, f32[1152]{0:T(1024)}, u32[]{:S(2)}) copy-start(f32[1152]{0:T(1024)} %get-tuple-element.138) | copy-start | bytes 13828
  1264.3 26.2 %copy-start.127 = (f32[1152]{0:T(1024)S(1)}, f32[1152]{0:T(1024)}, u32[]{:S(2)}) copy-start(f32[1152]{0:T(1024)} %get-tuple-element.140) | copy-start | bytes 13828
  1264.3 229.5 %all-gather.4.cloned.1.call-start = ((), (), s32[]{:S(2)}) async-start(), calls=%async_computation.10 | async-start | bytes 2580480 | tf_op jit(solution)/shard_map/all_gather | solution.py:333
  1264.9 284.4 %all-gather.8.cloned.1.call-start = ((), (), s32[]{:S(2)}) async-start(), calls=%async_computation.14 | async-start | bytes 3317760 | tf_op jit(solution)/shard_map/all_gather | solution.py:342
  1289.7 315.1 %all-gather.6.cloned.1.call-start = ((), (), s32[]{:S(2)}) async-start(), calls=%async_computation.12 | async-start | bytes 3317760 | tf_op jit(solution)/shard_map/all_gather | solution.py:339
  1336.5 58.1 %copy-start.130 = (f32[1152]{0:T(1024)S(1)}, f32[1152]{0:T(1024)}, u32[]{:S(2)}) copy-start(f32[1152]{0:T(1024)} %get-tuple-element.88) | copy-start | bytes 13828
  1336.5 58.1 %copy-start.131 = (f32[1152]{0:T(1024)S(1)}, f32[1152]{0:T(1024)}, u32[]{:S(2)}) copy-start(f32[1152]{0:T(1024)} %get-tuple-element.108) | copy-start | bytes 13828
  1336.5 58.1 %copy-start.134 = (f32[1152]{0:T(1024)S(1)}, f32[1152]{0:T(1024)}, u32[]{:S(2)}) copy-start(f32[1152]{0:T(1024)} %get-tuple-element.90) | copy-start | bytes 13828
  1336.5 58.1 %copy-start.135 = (f32[1152]{0:T(1024)S(1)}, f32[1152]{0:T(1024)}, u32[]{:S(2)}) copy-start(f32[1152]{0:T(1024)} %get-tuple-element.109) | copy-start | bytes 13828
  1336.5 80.5 %copy-start.109 = (f32[1152]{0:T(1024)S(1)}, f32[1152]{0:T(1024)}, u32[]{:S(2)}) copy-start(f32[1152]{0:T(1024)} %copy-done.108) | copy-start | bytes 13828
  (147 other events, 664.1 us)
Sparse Core Ops, SparseCore 0:
  27.3 47.6 all-reduce.17
  94.1 44.9 all-reduce.19
  201.9 46.4 all-reduce.21
  284.3 72.6 all-reduce.37
  444.9 73.7 all-reduce.35
  606.3 71.8 all-reduce.33
  777.1 73.7 all-reduce.31
  912.2 44.1 all-reduce.23
  998.5 44.9 all-reduce.25
  1103.1 44.0 all-reduce.27
  1191.8 43.1 reduce-scatter.12
  1237.7 51.9 reduce-scatter.10
  1292.0 24.2 reduce-scatter.14
  1319.3 71.6 all-reduce.29
  1393.7 53.6 reduce-scatter.8
  1448.9 44.8 all-gather.3
  1495.2 54.0 all-gather.7
  1550.8 54.0 all-gather.5
where the time goes:
time: 1640 us; the launch traced here: 1630 us
  waiting for transfers between devices  980 us (60%)
  matrix products  304 us (19%)
  other arithmetic  195 us (12%)
  local copies, waits for them, and re-layouts  72 us (4%)
  blocking collectives  41.1 us (3%)
  starting transfers between devices  19.7 us (1%)
  between operations  17.4 us (1%)
    psum x4, waiting for transfers between devices, layer_backward(): lax.psum(jnp.einsum('sc,dc->sd', d_packed, w_qkv, preferred_element_type=...  229 us
    psum x4, waiting for transfers between devices, layer_backward(): lax.psum(jnp.einsum('sf,df->sd', d_pre, w_fc1, preferred_element_type=jnp...  214 us
    ppermute x6, waiting for transfers between devices, shifted(): return lax.ppermute(value, axis, pairs)  199 us
    psum x2, waiting for transfers between devices, layer_forward(): lax.psum(jnp.dot(mixed_low, w_out, preferred_element_type=jnp.float32).as...  93.8 us
    unnamed x378, local copies, waits for them, and re-layouts  62.6 us
    dot_general x4, matrix products, layer_forward(): jnp.dot(act_out.astype(jnp.bfloat16), w_fc2, preferred_element_type=jnp.f...  55.3 us
    all_gather x1, waiting for transfers between devices, on_device(): lax.all_gather(share_list[3].astype(jnp.bfloat16), 'dp', axis=1, tiled=True)  47.7 us
    psum x1, waiting for transfers between devices, layer_forward(): lax.psum(jnp.dot(act_out.astype(jnp.bfloat16), w_fc2, preferred_element_t...  45 us
  transfers between devices with their start and end apart: 24, of which 23 were waited for; matrix products, arithmetic and copies ran while one was open for 10% of the time, Pallas kernels for 0%

commit v1 on v0

--- a/solution.py
+++ b/solution.py
@@ -7,6 +7,24 @@
 EPSILON = 1e-06
 GELU_SCALE = 0.7978845608028654
 GELU_CUBIC = 0.044715
+
+
+def gather_around(shard, axis, dim):
+    ways, here, step = (lax.axis_size(axis), lax.axis_index(axis), shard.shape[dim])
+    dims = [n * ways if d == dim else n for d, n in enumerate(shard.shape)]
+    full = lax.dynamic_update_slice_in_dim(
+        jnp.zeros(dims, shard.dtype), shard, here * step, axis=dim
+    )
+    going_up = going_down = shard
+    for far in range(1, ways // 2 + 1):
+        going_up = lax.ppermute(going_up, axis, [(d, (d + 1) % ways) for d in range(ways)])
+        full = lax.dynamic_update_slice_in_dim(full, going_up, (here - far) % ways * step, axis=dim)
+        if 2 * far < ways:
+            going_down = lax.ppermute(going_down, axis, [(d, (d - 1) % ways) for d in range(ways)])
+            full = lax.dynamic_update_slice_in_dim(
+                full, going_down, (here + far) % ways * step, axis=dim
+            )
+    return full
 
 
 def shifted(value, axis, by):
@@ -339,9 +357,7 @@
         lax.all_gather(share_list[2].astype(jnp.bfloat16), "dp", axis=0, tiled=True).astype(
             jnp.float32
         ),
-        lax.all_gather(share_list[3].astype(jnp.bfloat16), "dp", axis=1, tiled=True).astype(
-            jnp.float32
-        ),
+        gather_around(share_list[3].astype(jnp.bfloat16), "dp", 1).astype(jnp.float32),
     )
     small = lax.psum(
         (totals[0], totals[1], totals[3], totals[5], totals[6], totals[7], totals[9], totals[11]),

time: 1640 us -> 2260 us (1.38)
  local copies, waits for them, and re-layouts: 72 us -> 708 us
  waiting for transfers between devices: 980 us -> 887 us
  blocking collectives: 41.1 us -> 73.5 us
  starting transfers between devices: 19.7 us -> 43.3 us
    dynamic_update_slice x0 -> x4, local copies, waits for them, and re-layouts: none -> 629 us  [the longest x2 379 us: gather_around(): lax.dynamic_update_slice_in_dim(full, going_up, (here - far) % ways * ste...]
    all_gather x1 -> x0, waiting for transfers between devices: 47.7 us -> none  [on_device(): lax.all_gather(share_list[3].astype(jnp.bfloat16), 'dp', axis=1, tiled=True)]
    all_gather x1, waiting for transfers between devices: 38.3 us -> 0.01 us  [on_device(): lax.all_gather(share_list[2].astype(jnp.bfloat16), 'dp', axis=0, tiled=True)]
    all_gather x1, waiting for transfers between devices: 37.6 us -> 0.01 us  [on_device(): lax.all_gather(share_list[0].astype(jnp.bfloat16), 'dp', axis=0, tiled=True)]
    unnamed x19 -> x18, waiting for transfers between devices: 26.4 us -> 0.78 us
    ppermute x0 -> x3, starting transfers between devices: none -> 23.9 us  [the longest x2 20.5 us: gather_around(): lax.ppermute(going_up, axis, [(d, (d + 1) % ways) for d in range(ways)])]
    psum x4, waiting for transfers between devices: 229 us -> 252 us  [layer_backward(): lax.psum(jnp.einsum('sc,dc->sd', d_packed, w_qkv, preferred_element_type=...]
    reduce_scatter x1, waiting for transfers between devices: 24.7 us -> 48.1 us  [on_device(): lax.psum_scatter(totals[10].astype(jnp.bfloat16), 'dp', scatter_dimension...]
  transfers between devices with their start and end apart: 24 -> 26, of which waited for: 23 -> 20; matrix products, arithmetic and copies ran while one was open for 10% -> 37% of each run, Pallas kernels for 0% -> 0%
where the time goes in v1:
time: 2260 us; the launch traced here: 2240 us
  waiting for transfers between devices  887 us (39%)
  local copies, waits for them, and re-layouts  708 us (31%)
  matrix products  313 us (14%)
  other arithmetic  198 us (9%)
  blocking collectives  73.5 us (3%)
  starting transfers between devices  43.3 us (2%)
    dynamic_update_slice x2, local copies, waits for them, and re-layouts, gather_around(): lax.dynamic_update_slice_in_dim(full, going_up, (here - far) % ways * ste...  379 us
    psum x4, waiting for transfers between devices, layer_backward(): lax.psum(jnp.einsum('sc,dc->sd', d_packed, w_qkv, preferred_element_type=...  252 us
    psum x4, waiting for transfers between devices, layer_backward(): lax.psum(jnp.einsum('sf,df->sd', d_pre, w_fc1, preferred_element_type=jnp...  214 us
    ppermute x6, waiting for transfers between devices, shifted(): return lax.ppermute(value, axis, pairs)  199 us
    dynamic_update_slice x1, local copies, waits for them, and re-layouts, gather_around(): lax.dynamic_update_slice_in_dim(full, going_down, (here + far) % ways * s...  190 us
    psum x2, waiting for transfers between devices, layer_forward(): lax.psum(jnp.dot(mixed_low, w_out, preferred_element_type=jnp.float32).as...  93.7 us
    dynamic_update_slice x1, local copies, waits for them, and re-layouts, gather_around(): lax.dynamic_update_slice_in_dim(jnp.zeros(dims, shard.dtype), shard, here...  60.4 us
    dot_general x4, matrix products, layer_forward(): jnp.dot(act_out.astype(jnp.bfloat16), w_fc2, preferred_element_type=jnp.f...  55.1 us
  transfers between devices with their start and end apart: 26, of which 20 were waited for; matrix products, arithmetic and copies ran while one was open for 37% of the time, Pallas kernels for 0%

profile of v1, /device:TPU:0, one launch (start us, length us, event | category | flops | bytes accessed | tf_op | source)
XLA Modules:
  0.0 2240.4 jit_solution(4801928994172790844)
XLA Ops:
  27.5 47.4 %all-reduce.18.cloned.1.call-done = bf16[729,1152]{1,0:T(8,128)(2,1)} async-done(((bf16[729,1152]{1,0:T(8,128)(2,1)}), bf16[729,1152]{1,0:T(8,128)(2,1)}) %all-reduce.18.cloned.1.call-update) | async-done | bytes 1679632 | tf_op jit(solution)/shard_map/psum | solution.py:166
  80.3 13.7 convolution_convert_fusion.15
  94.1 45.0 %all-reduce.20.cloned.1.call-done = bf16[729,1152]{1,0:T(8,128)(2,1)} async-done(((bf16[729,1152]{1,0:T(8,128)(2,1)}), bf16[729,1152]{1,0:T(8,128)(2,1)}) %all-reduce.20.cloned.1.call-update) | async-done | bytes 1679632 | tf_op jit(solution)/shard_map/psum | solution.py:176
  143.7 4.8 collective-permute-start
  148.5 35.0 %collective-permute-done = bf16[729,1152]{1,0:T(8,128)(2,1)} collective-permute-done((bf16[729,1152]{1,0:T(8,128)(2,1)}, bf16[729,1152]{1,0:T(8,128)(2,1)}, u32[]{:S(2)}, u32[]{:S(2)}) %collective-permute-start) | collective-permute-done | bytes 1679648 | tf_op jit(solution)/shard_map/ppermute | solution.py:33
  202.2 46.2 %all-reduce.22.cloned.1.call-done = bf16[729,1152]{1,0:T(8,128)(2,1)} async-done(((bf16[729,1152]{1,0:T(8,128)(2,1)}), bf16[729,1152]{1,0:T(8,128)(2,1)}) %all-reduce.22.cloned.1.call-update) | async-done | bytes 1679632 | tf_op jit(solution)/shard_map/psum | solution.py:166
  258.2 7.0 convert_reduce_fusion.23
  270.2 13.9 convolution_convert_fusion.12
  284.2 72.7 %all-reduce.38.cloned.1.call-done = (bf16[729,1152]{1,0:T(8,128)(2,1)}, bf16[729,1152]{1,0:T(8,128)(2,1)}) async-done(((bf16[729,1152]{1,0:T(8,128)(2,1)}, bf16[729,1152]{1,0:T(8,128)(2,1)}), (bf16[729,1152]{1,0:T(8,128)(2,1)}, bf16[729,1152]{1,0:T(8,128)(2,1)})) %all-reduce.38.cloned.1.call-update) | async-done | bytes 3359248 | tf_op jit(solution)/shard_map/psum | solution.py:223
  369.6 30.2 %collective-permute-done.2 = bf16[729,1152]{1,0:T(8,128)(2,1)S(1)} collective-permute-done((bf16[729,1152]{1,0:T(8,128)(2,1)S(1)}, bf16[729,1152]{1,0:T(8,128)(2,1)S(1)}, u32[]{:S(2)}, u32[]{:S(2)}) %collective-permute-start.2) | collective-permute-done | bytes 1679648 | tf_op jit(solution)/shard_map/ppermute | solution.py:33
  408.2 4.9 multiply_reduce_fusion.3
  413.1 10.2 multiply_convert_fusion.3
  447.3 71.8 %all-reduce.36.cloned.1.call-done = (bf16[729,1152]{1,0:T(8,128)(2,1)}, bf16[729,1152]{1,0:T(8,128)(2,1)}) async-done(((bf16[729,1152]{1,0:T(8,128)(2,1)}, bf16[729,1152]{1,0:T(8,128)(2,1)}), (bf16[729,1152]{1,0:T(8,128)(2,1)}, bf16[729,1152]{1,0:T(8,128)(2,1)})) %all-reduce.36.cloned.1.call-update) | async-done | bytes 3359248 | tf_op jit(solution)/shard_map/psum | solution.py:238
  531.1 36.7 %collective-permute-done.1 = bf16[729,1152]{1,0:T(8,128)(2,1)} collective-permute-done((bf16[729,1152]{1,0:T(8,128)(2,1)}, bf16[729,1152]{1,0:T(8,128)(2,1)}, u32[]{:S(2)}, u32[]{:S(2)}) %collective-permute-start.1) | collective-permute-done | bytes 1679648 | tf_op jit(solution)/shard_map/ppermute | solution.py:33
  567.8 6.8 fusion.440
  576.9 13.7 convolution_convert_fusion.9
  595.3 5.8 convert_reduce_fusion.22
  606.2 71.9 %all-reduce.34.cloned.1.call-done = (bf16[729,1152]{1,0:T(8,128)(2,1)}, bf16[729,1152]{1,0:T(8,128)(2,1)}) async-done(((bf16[729,1152]{1,0:T(8,128)(2,1)}, bf16[729,1152]{1,0:T(8,128)(2,1)}), (bf16[729,1152]{1,0:T(8,128)(2,1)}, bf16[729,1152]{1,0:T(8,128)(2,1)})) %all-reduce.34.cloned.1.call-update) | async-done | bytes 3359248 | tf_op jit(solution)/shard_map/psum | solution.py:223
  691.7 29.6 %collective-permute-done.4 = bf16[729,1152]{1,0:T(8,128)(2,1)S(1)} collective-permute-done((bf16[729,1152]{1,0:T(8,128)(2,1)S(1)}, bf16[729,1152]{1,0:T(8,128)(2,1)S(1)}, u32[]{:S(2)}, u32[]{:S(2)}) %collective-permute-start.4) | collective-permute-done | bytes 1679648 | tf_op jit(solution)/shard_map/ppermute | solution.py:33
  742.8 4.9 multiply_reduce_fusion.2
  747.6 10.2 multiply_convert_fusion.2
  763.4 6.7 broadcast_select_fusion.11
  783.4 4.9 fusion.452
  788.2 62.6 %all-reduce.32.cloned.1.call-done = (bf16[729,1152]{1,0:T(8,128)(2,1)}, bf16[729,1152]{1,0:T(8,128)(2,1)}) async-done(((bf16[729,1152]{1,0:T(8,128)(2,1)}, bf16[729,1152]{1,0:T(8,128)(2,1)}), (bf16[729,1152]{1,0:T(8,128)(2,1)}, bf16[729,1152]{1,0:T(8,128)(2,1)})) %all-reduce.32.cloned.1.call-update) | async-done | bytes 3359248 | tf_op jit(solution)/shard_map/psum | solution.py:238
  866.2 32.6 %collective-permute-done.3 = bf16[729,1152]{1,0:T(8,128)(2,1)S(1)} collective-permute-done((bf16[729,1152]{1,0:T(8,128)(2,1)S(1)}, bf16[729,1152]{1,0:T(8,128)(2,1)S(1)}, u32[]{:S(2)}, u32[]{:S(2)}) %collective-permute-start.3) | collective-permute-done | bytes 1679648 | tf_op jit(solution)/shard_map/ppermute | solution.py:33
  901.4 5.6 convert_reduce_fusion.21
  912.4 6.2 fusion.453
  922.9 33.5 %all-reduce.24.cloned.1.call-done = bf16[729,1152]{1,0:T(8,128)(2,1)} async-done(((bf16[729,1152]{1,0:T(8,128)(2,1)}), bf16[729,1152]{1,0:T(8,128)(2,1)}) %all-reduce.24.cloned.1.call-update) | async-done | bytes 1679632 | tf_op jit(solution)/shard_map/psum | solution.py:223
  956.4 4.7 fusion.151
  967.1 6.6 convert_reduce_fusion.26
  973.8 4.7 multiply_reduce_fusion.1
  978.5 10.2 multiply_convert_fusion.1
  1000.7 42.8 %all-reduce.26.cloned.1.call-done = bf16[729,1152]{1,0:T(8,128)(2,1)} async-done(((bf16[729,1152]{1,0:T(8,128)(2,1)}), bf16[729,1152]{1,0:T(8,128)(2,1)}) %all-reduce.26.cloned.1.call-update) | async-done | bytes 1679632 | tf_op jit(solution)/shard_map/psum | solution.py:238
  1056.3 34.5 %collective-permute-done.5 = bf16[729,1152]{1,0:T(8,128)(2,1)S(1)} collective-permute-done((bf16[729,1152]{1,0:T(8,128)(2,1)S(1)}, bf16[729,1152]{1,0:T(8,128)(2,1)S(1)}, u32[]{:S(2)}, u32[]{:S(2)}) %collective-permute-start.5) | collective-permute-done | bytes 1679648 | tf_op jit(solution)/shard_map/ppermute | solution.py:33
  1092.9 5.0 convert_reduce_fusion.20
  1105.5 6.2 fusion.235
  1111.7 35.5 %all-reduce.28.cloned.1.call-done = bf16[729,1152]{1,0:T(8,128)(2,1)} async-done(((bf16[729,1152]{1,0:T(8,128)(2,1)}), bf16[729,1152]{1,0:T(8,128)(2,1)}) %all-reduce.28.cloned.1.call-update) | async-done | bytes 1679632 | tf_op jit(solution)/shard_map/psum | solution.py:223
  1156.7 5.4 convert_reduce_fusion.24
  1162.2 4.8 multiply_reduce_fusion
  1167.0 10.2 multiply_convert_fusion
  1192.0 7.8 fusion.432
  1203.6 5.3 fusion.433
  1213.1 8.8 fusion.1
  1227.0 7.4 convolution_select_fusion.1
  1234.5 13.8 convolution_convert_fusion.4
  1248.2 7.8 fusion.295
  1259.4 5.3 convolution_select_fusion
  1264.8 8.6 fusion.5
  1275.3 34.3 %all_gather.10 = bf16[288,1152]{0,1:T(8,128)(2,1)S(1)} all-gather(bf16[288,288]{0,1:T(8,128)(2,1)} %bitcast.468), channel_id=1, replica_groups=mesh['pipe'=2,'dp'=4,'mp'=4] {'dp'}, dimensions={1}, use_global_device_ids=true | all-gather | bytes 829440 | tf_op jit(solution)/shard_map/all_gather | solution.py:354
  1314.0 15.9 reduce-scatter.9.cloned.1.call-done
  1329.9 75.1 %all-reduce.30.cloned.1.call-done = (bf16[729,1152]{1,0:T(8,128)(2,1)}, bf16[729,1152]{1,0:T(8,128)(2,1)}) async-done(((bf16[729,1152]{1,0:T(8,128)(2,1)}, bf16[729,1152]{1,0:T(8,128)(2,1)}), (bf16[729,1152]{1,0:T(8,128)(2,1)}, bf16[729,1152]{1,0:T(8,128)(2,1)})) %all-reduce.30.cloned.1.call-update) | async-done | bytes 3359248 | tf_op jit(solution)/shard_map/psum | solution.py:238
  1412.5 48.1 %reduce-scatter.11.cloned.1.call-done = bf16[1076,288]{0,1:T(8,128)(2,1)} async-done(((bf16[1076,1152]{0,1:T(8,128)(2,1)}), bf16[1076,288]{0,1:T(8,128)(2,1)}) %reduce-scatter.11.cloned.1.call-update) | async-done | bytes 619792 | tf_op jit(solution)/shard_map/reduce_scatter | solution.py:346
  1468.0 19.1 collective-permute-done.6
  1487.0 20.0 collective-permute-start.8
  1511.8 39.1 %all-reduce = (f32[1,1152]{1,0:T(1,128)}, f32[1,1152]{1,0:T(1,128)}, f32[1,2,288]{2,1,0:T(2,128)}, f32[1,1152]{1,0:T(1,128)}, f32[1,1152]{1,0:T(1,128)}, /*index...) all-reduce(f32[1,1152]{1,0:T(1,128)S(1)} %broadcast_in_dim.109, ...), channel_id=1, replica_groups=mesh['pipe'=2,'dp'=4,'mp'=4] {'dp'}, use_global_device_ids=true, to_apply=%region_80.81 | all-reduce | flops 8564 | bytes 68512 | tf_op jit(solution)/shard_map/psum | solution.py:362
  1558.3 60.4 %dynamic_update_slice.16 = bf16[1,1076,1152]{2,0,1:T(2,128)(2,1)} dynamic-update-slice(bf16[1,1076,1152]{2,0,1:T(2,128)(2,1)} %broadcast_in_dim.125, bf16[1,1076,288]{2,0,1:T(2,128)(2,1)} %copy.141, s32[]{:T(128)} %constant.138.clone.1, s32[]{:T(128)} %constant.138.clone.1, s32[]{:T(128)S(6)} %select_n.510) | dynamic-update-slice | bytes 1239556 | tf_op jit(solution)/shard_map/dynamic_update_slice | solution.py:15
  1618.7 4.7 copy.143
  1623.4 4.7 copy.142
  1628.1 189.2 %dynamic_update_slice.17 = bf16[1,1076,1152]{2,0,1:T(2,128)(2,1)} dynamic-update-slice(bf16[1,1076,1152]{2,0,1:T(2,128)(2,1)} %dynamic_update_slice.16, bf16[1,1076,288]{2,0,1:T(2,128)(2,1)} %copy.142, s32[]{:T(128)} %constant.138.clone.1, s32[]{:T(128)} %constant.138.clone.1, s32[]{:T(128)S(6)} %select_n.512) | dynamic-update-slice | bytes 1239556 | tf_op jit(solution)/shard_map/dynamic_update_slice | solution.py:21
  1817.3 189.8 %dynamic_update_slice.18 = bf16[1,1076,1152]{2,0,1:T(2,128)(2,1)} dynamic-update-slice(bf16[1,1076,1152]{2,0,1:T(2,128)(2,1)} %dynamic_update_slice.17, bf16[1,1076,288]{2,0,1:T(2,128)(2,1)} %copy.143, s32[]{:T(128)} %constant.138.clone.1, s32[]{:T(128)} %constant.138.clone.1, s32[]{:T(128)S(6)} %select_n.514) | dynamic-update-slice | bytes 1239556 | tf_op jit(solution)/shard_map/dynamic_update_slice | solution.py:24
  2007.1 4.7 copy.144
  2011.8 189.8 %dynamic_update_slice.19 = bf16[1,1076,1152]{2,0,1:T(2,128)(2,1)} dynamic-update-slice(bf16[1,1076,1152]{2,0,1:T(2,128)(2,1)} %dynamic_update_slice.18, bf16[1,1076,288]{2,0,1:T(2,128)(2,1)} %copy.144, s32[]{:T(128)} %constant.138.clone.1, s32[]{:T(128)} %constant.138.clone.1, s32[]{:T(128)S(6)} %select_n.516) | dynamic-update-slice | bytes 1239556 | tf_op jit(solution)/shard_map/dynamic_update_slice | solution.py:21
  2201.5 7.2 broadcast_in_dim.131
  2220.9 12.7 copy.146
  (627 shorter events, 338.5 us)
Async XLA Ops:
  7.2 73.1 %copy-start = (bf16[1,1152,1076]{1,2,0:T(8,128)(2,1)S(1)}, bf16[1,1152,1076]{1,2,0:T(8,128)(2,1)}, u32[]{:S(2)}) copy-start(bf16[1,1152,1076]{1,2,0:T(8,128)(2,1)} %param.22) | copy-start | bytes 7437316
  7.2 67.8 %all-reduce.18.cloned.1.call-start = ((), (), s32[]{:S(2)}) async-start(), calls=%async_computation.4 | async-start | bytes 3391488 | tf_op jit(solution)/shard_map/psum | solution.py:166
  27.2 112.0 %all-reduce.20.cloned.1.call-start = ((), (), s32[]{:S(2)}) async-start(), calls=%async_computation.5 | async-start | bytes 3391488 | tf_op jit(solution)/shard_map/psum | solution.py:176
  80.3 13.8 copy-start.151
  94.0 154.4 %all-reduce.22.cloned.1.call-start = ((), (), s32[]{:S(2)}) async-start(), calls=%async_computation.6 | async-start | bytes 3391488 | tf_op jit(solution)/shard_map/psum | solution.py:166
  94.1 584.0 %copy-start.109 = (f32[1152]{0:T(1024)}, f32[1152]{0:T(1024)S(1)}, u32[]{:S(2)}) copy-start(f32[1152]{0:T(1024)S(1)} %convert_reduce_fusion.32) | copy-start | bytes 13828
  143.7 39.8 %collective-permute-start = (bf16[729,1152]{1,0:T(8,128)(2,1)}, bf16[729,1152]{1,0:T(8,128)(2,1)}, u32[]{:S(2)}, u32[]{:S(2)}) collective-permute-start(bf16[729,1152]{1,0:T(8,128)(2,1)} %add_convert_fusion.10), channel_id=1, source_target_pairs={{0,16},{1,17},{2,18},{3,19},{4,20},{5,21},{6,22},{7,23},{8,24},{9,... | collective-permute-start | bytes 5038856 | tf_op jit(solution)/shard_map/ppermute | solution.py:33
  201.8 155.2 %all-reduce.38.cloned.1.call-start = ((), (), s32[]{:S(2)}) async-start(), calls=%async_computation.20 | async-start | bytes 6782976 | tf_op jit(solution)/shard_map/psum | solution.py:223
  255.1 144.8 %copy-start.111 = (f32[729]{0:T(1024)}, f32[729]{0:T(1024)S(1)}, u32[]{:S(2)}) copy-start(f32[729]{0:T(1024)S(1)} %broadcast_multiply_fusion.28) | copy-start | bytes 8752
  255.6 144.3 %copy-start.117 = (f32[729]{0:T(1024)}, f32[729]{0:T(1024)S(1)}, u32[]{:S(2)}) copy-start(f32[729]{0:T(1024)S(1)} %add_rsqrt_fusion.12) | copy-start | bytes 8752
  284.1 234.9 %all-reduce.36.cloned.1.call-start = ((), (), s32[]{:S(2)}) async-start(), calls=%async_computation.19 | async-start | bytes 6782976 | tf_op jit(solution)/shard_map/psum | solution.py:238
  360.4 39.5 %collective-permute-start.2 = (bf16[729,1152]{1,0:T(8,128)(2,1)S(1)}, bf16[729,1152]{1,0:T(8,128)(2,1)S(1)}, u32[]{:S(2)}, u32[]{:S(2)}) collective-permute-start(bf16[729,1152]{1,0:T(8,128)(2,1)S(1)} %add_convert_fusion.7), channel_id=1, source_target_pairs={{0,16},{1,17},{2,18},{3,19},{4,20},{5,21},{6,22},{7,23},{8,24},{9,... | collective-permute-start | bytes 5038856 | tf_op jit(solution)/shard_map/ppermute | solution.py:33
  364.2 35.6 %slice-start = ((s8[5087232]{0:T(1024)(128)(4,1)}), s8[4194304]{0:T(1024)(128)(4,1)S(1)}, s32[]{:S(2)}) async-start(s8[5087232]{0:T(1024)(128)(4,1)} %bitcast.391), calls=%async_computation.21 | async-start | bytes 8388608
  364.2 35.6 %slice-start.1 = ((s8[5087232]{0:T(1024)(128)(4,1)}), s8[892928]{0:T(1024)(128)(4,1)S(1)}, s32[]{:S(2)}) async-start(s8[5087232]{0:T(1024)(128)(4,1)} %bitcast.391), calls=%async_computation.22 | async-start | bytes 1785856
  365.7 42.5 %copy-start.1 = (f32[4,729,729]{1,2,0:T(8,128)}, f32[4,729,729]{1,2,0:T(8,128)S(1)}, u32[]{:S(2)}) copy-start(f32[4,729,729]{1,2,0:T(8,128)S(1)} %fusion.450) | copy-start | bytes 25509172
  445.1 233.0 %all-reduce.34.cloned.1.call-start = ((), (), s32[]{:S(2)}) async-start(), calls=%async_computation.18 | async-start | bytes 6782976 | tf_op jit(solution)/shard_map/psum | solution.py:223
  445.2 81.9 %copy-start.115 = (f32[729]{0:T(1024)}, f32[729]{0:T(1024)S(1)}, u32[]{:S(2)}) copy-start(f32[729]{0:T(1024)S(1)} %broadcast_multiply_fusion.25) | copy-start | bytes 8752
  447.2 79.8 %copy-start.121 = (f32[729]{0:T(1024)}, f32[729]{0:T(1024)S(1)}, u32[]{:S(2)}) copy-start(f32[729]{0:T(1024)S(1)} %add_rsqrt_fusion.11) | copy-start | bytes 8752
  527.0 40.8 %collective-permute-start.1 = (bf16[729,1152]{1,0:T(8,128)(2,1)}, bf16[729,1152]{1,0:T(8,128)(2,1)}, u32[]{:S(2)}, u32[]{:S(2)}) collective-permute-start(bf16[729,1152]{1,0:T(8,128)(2,1)} %fusion.121), channel_id=1, source_target_pairs={{16,0},{17,1},{18,2},{19,3},{20,4},{21,5},{22,6},{23,7},{24,8},{25... | collective-permute-start | bytes 5038856 | tf_op jit(solution)/shard_map/ppermute | solution.py:33
  528.3 39.5 %copy-start.4 = (bf16[729,1152]{1,0:T(8,128)(2,1)S(1)}, bf16[729,1152]{1,0:T(8,128)(2,1)}, u32[]{:S(2)}) copy-start(bf16[729,1152]{1,0:T(8,128)(2,1)} %get-tuple-element.155) | copy-start | bytes 5038852
  528.4 39.5 %copy-start.41 = (bf16[729,1152]{1,0:T(8,128)(2,1)S(1)}, bf16[729,1152]{1,0:T(8,128)(2,1)}, u32[]{:S(2)}) copy-start(bf16[729,1152]{1,0:T(8,128)(2,1)} %all-reduce.18.cloned.1.call-done) | copy-start | bytes 5038852
  574.6 112.8 %copy-start.113 = (f32[729]{0:T(1024)}, f32[729]{0:T(1024)S(1)}, u32[]{:S(2)}) copy-start(f32[729]{0:T(1024)S(1)} %broadcast_multiply_fusion.20) | copy-start | bytes 8752
  576.8 110.6 %copy-start.119 = (f32[729]{0:T(1024)}, f32[729]{0:T(1024)S(1)}, u32[]{:S(2)}) copy-start(f32[729]{0:T(1024)S(1)} %add_rsqrt_fusion.8) | copy-start | bytes 8752
  606.1 244.8 %all-reduce.32.cloned.1.call-start = ((), (), s32[]{:S(2)}) async-start(), calls=%async_computation.17 | async-start | bytes 6782976 | tf_op jit(solution)/shard_map/psum | solution.py:238
  681.6 39.7 %collective-permute-start.4 = (bf16[729,1152]{1,0:T(8,128)(2,1)S(1)}, bf16[729,1152]{1,0:T(8,128)(2,1)S(1)}, u32[]{:S(2)}, u32[]{:S(2)}) collective-permute-start(bf16[729,1152]{1,0:T(8,128)(2,1)S(1)} %add_convert_fusion.4), channel_id=1, source_target_pairs={{0,16},{1,17},{2,18},{3,19},{4,20},{5,21},{6,22},{7,23},{8,24},{9,... | collective-permute-start | bytes 5038856 | tf_op jit(solution)/shard_map/ppermute | solution.py:33
  690.0 31.4 %copy-start.5 = (bf16[729,1152]{1,0:T(8,128)(2,1)S(1)}, bf16[729,1152]{1,0:T(8,128)(2,1)}, u32[]{:S(2)}) copy-start(bf16[729,1152]{1,0:T(8,128)(2,1)} %get-tuple-element.155) | copy-start | bytes 5038852
  777.0 179.5 %all-reduce.24.cloned.1.call-start = ((), (), s32[]{:S(2)}) async-start(), calls=%async_computation.7 | async-start | bytes 3391488 | tf_op jit(solution)/shard_map/psum | solution.py:223
  858.2 40.6 %collective-permute-start.3 = (bf16[729,1152]{1,0:T(8,128)(2,1)S(1)}, bf16[729,1152]{1,0:T(8,128)(2,1)S(1)}, u32[]{:S(2)}, u32[]{:S(2)}) collective-permute-start(bf16[729,1152]{1,0:T(8,128)(2,1)S(1)} %fusion.114), channel_id=1, source_target_pairs={{16,0},{17,1},{18,2},{19,3},{20,4},{21,5},{22,6},{23,7},{24,8},{25... | collective-permute-start | bytes 5038856 | tf_op jit(solution)/shard_map/ppermute | solution.py:33
  866.2 40.8 %copy-start.173 = (f32[729,1076]{0,1:T(8,128)}, f32[729,1076]{0,1:T(8,128)S(1)}, u32[]{:S(2)}) copy-start(f32[729,1076]{0,1:T(8,128)S(1)} %convolution_add_fusion.3) | copy-start | bytes 9412852
  866.2 35.2 %copy-start.154 = (bf16[1,1076,1152]{2,1,0:T(8,128)(2,1)S(1)}, bf16[1,1076,1152]{2,1,0:T(8,128)(2,1)}, u32[]{:S(2)}) copy-start(bf16[1,1076,1152]{2,1,0:T(8,128)(2,1)} %param.24) | copy-start | bytes 7437316
  912.1 131.3 %all-reduce.26.cloned.1.call-start = ((), (), s32[]{:S(2)}) async-start(), calls=%async_computation.8 | async-start | bytes 3391488 | tf_op jit(solution)/shard_map/psum | solution.py:238
  961.2 12.6 slice-start.5
  961.2 12.6 slice-start.6
  998.4 148.8 %all-reduce.28.cloned.1.call-start = ((), (), s32[]{:S(2)}) async-start(), calls=%async_computation.9 | async-start | bytes 3391488 | tf_op jit(solution)/shard_map/psum | solution.py:223
  1050.2 40.7 %collective-permute-start.5 = (bf16[729,1152]{1,0:T(8,128)(2,1)S(1)}, bf16[729,1152]{1,0:T(8,128)(2,1)S(1)}, u32[]{:S(2)}, u32[]{:S(2)}) collective-permute-start(bf16[729,1152]{1,0:T(8,128)(2,1)S(1)} %fusion.107), channel_id=1, source_target_pairs={{16,0},{17,1},{18,2},{19,3},{20,4},{21,5},{22,6},{23,7},{24,8},{25... | collective-permute-start | bytes 5038856 | tf_op jit(solution)/shard_map/ppermute | solution.py:33
  1056.3 41.6 %copy-start.175 = (f32[729,1076]{0,1:T(8,128)}, f32[729,1076]{0,1:T(8,128)S(1)}, u32[]{:S(2)}) copy-start(f32[729,1076]{0,1:T(8,128)S(1)} %convolution_add_fusion.2) | copy-start | bytes 9412852
  1056.3 36.6 %copy-start.155 = (bf16[1,1076,1152]{2,1,0:T(8,128)(2,1)S(1)}, bf16[1,1076,1152]{2,1,0:T(8,128)(2,1)}, u32[]{:S(2)}) copy-start(bf16[1,1076,1152]{2,1,0:T(8,128)(2,1)} %param.24) | copy-start | bytes 7437316
  1103.0 170.7 %reduce-scatter.13.cloned.1.call-start = ((), (), s32[]{:S(2)}) async-start(), calls=%async_computation.14 | async-start | bytes 2580480 | tf_op jit(solution)/shard_map/reduce_scatter | solution.py:337
  1151.3 10.8 slice-start.2
  1151.4 10.8 slice-start.3
  1167.0 10.3 copy-start.75
  1191.7 83.5 %reduce-scatter.15.cloned.1.call-start = ((), (), s32[]{:S(2)}) async-start(), calls=%async_computation.15 | async-start | bytes 1105920
  1213.0 116.9 %reduce-scatter.9.cloned.1.call-start = ((), (), s32[]{:S(2)}) async-start(), calls=%async_computation.11 | async-start | bytes 3317760 | tf_op jit(solution)/shard_map/reduce_scatter | solution.py:343
  1226.6 178.5 %all-reduce.30.cloned.1.call-start = ((), (), s32[]{:S(2)}) async-start(), calls=%async_computation.16 | async-start | bytes 6782976 | tf_op jit(solution)/shard_map/psum | solution.py:238
  1259.3 201.2 %reduce-scatter.11.cloned.1.call-start = ((), (), s32[]{:S(2)}) async-start(), calls=%async_computation.13 | async-start | bytes 3317760 | tf_op jit(solution)/shard_map/reduce_scatter | solution.py:346
  1264.7 9.5 copy-start.139
  1264.7 9.6 copy-start.140
  1264.7 9.7 copy-start.141
  1264.7 9.8 copy-start.142
  1264.8 9.8 copy-start.143
  1264.8 10.0 copy-start.123
  1264.8 10.0 copy-start.125
  1264.8 10.0 copy-start.127
  1273.6 935.2 %all-gather.3.cloned.1.call-start = ((), (), s32[]{:S(2)}) async-start(), calls=%async_computation.10 | async-start | bytes 2580480 | tf_op jit(solution)/shard_map/all_gather | solution.py:351
  1274.1 942.4 %all-gather.5.cloned.1.call-start = ((), (), s32[]{:S(2)}) async-start(), calls=%async_computation.12 | async-start | bytes 3317760 | tf_op jit(solution)/shard_map/all_gather | solution.py:357
  1408.8 52.3 %copy-start.110 = (f32[1152]{0:T(1024)S(1)}, f32[1152]{0:T(1024)}, u32[]{:S(2)}) copy-start(f32[1152]{0:T(1024)} %copy-done.109) | copy-start | bytes 13828
  1460.6 26.5 %collective-permute-start.6 = (bf16[1076,288]{0,1:T(8,128)(2,1)}, bf16[1076,288]{0,1:T(8,128)(2,1)}, u32[]{:S(2)}, u32[]{:S(2)}) collective-permute-start(bf16[1076,288]{0,1:T(8,128)(2,1)} %reduce-scatter.11.cloned.1.call-done), channel_id=1, source_target_pairs={{0,4},{4,8},{8,12},{12,0},{1,5},{5,9},{9,13},{13,1},{2,6},{6,10},{... | collective-permute-start | bytes 1859336 | tf_op jit(solution)/shard_map/ppermute | solution.py:20
  1461.1 45.9 %copy-start.55 = (bf16[729,1152]{1,0:T(8,128)(2,1)S(1)}, bf16[729,1152]{1,0:T(8,128)(2,1)}, u32[]{:S(2)}) copy-start(bf16[729,1152]{1,0:T(8,128)(2,1)} %copy-done.54) | copy-start | bytes 5038852
  1461.1 45.9 %copy-start.57 = (bf16[729,1152]{1,0:T(8,128)(2,1)S(1)}, bf16[729,1152]{1,0:T(8,128)(2,1)}, u32[]{:S(2)}) copy-start(bf16[729,1152]{1,0:T(8,128)(2,1)} %copy-done.56) | copy-start | bytes 5038852
  1461.1 45.9 %copy-start.59 = (bf16[729,1152]{1,0:T(8,128)(2,1)S(1)}, bf16[729,1152]{1,0:T(8,128)(2,1)}, u32[]{:S(2)}) copy-start(bf16[729,1152]{1,0:T(8,128)(2,1)} %copy-done.58) | copy-start | bytes 5038852
  1461.1 45.9 %copy-start.61 = (bf16[729,1152]{1,0:T(8,128)(2,1)S(1)}, bf16[729,1152]{1,0:T(8,128)(2,1)}, u32[]{:S(2)}) copy-start(bf16[729,1152]{1,0:T(8,128)(2,1)} %copy-done.60) | copy-start | bytes 5038852
  1464.6 154.1 %collective-permute-start.7 = (bf16[1076,288]{0,1:T(8,128)(2,1)}, bf16[1076,288]{0,1:T(8,128)(2,1)}, u32[]{:S(2)}, u32[]{:S(2)}) collective-permute-start(bf16[1076,288]{0,1:T(8,128)(2,1)} %reduce-scatter.11.cloned.1.call-done), channel_id=1, source_target_pairs={{0,12},{4,0},{8,4},{12,8},{1,13},{5,1},{9,5},{13,9},{2,14},{6,2},{... | collective-permute-start | bytes 1859336 | tf_op jit(solution)/shard_map/ppermute | solution.py:23
  1487.0 520.1 %collective-permute-start.8 = (bf16[1076,288]{0,1:T(8,128)(2,1)}, bf16[1076,288]{0,1:T(8,128)(2,1)}, u32[]{:S(2)}, u32[]{:S(2)}) collective-permute-start(bf16[1076,288]{0,1:T(8,128)(2,1)} %collective-permute-done.6), channel_id=1, source_target_pairs={{0,4},{4,8},{8,12},{12,0},{1,5},{5,9},{9,13},{13,1},{2,6},{6,10},{... | collective-permute-start | bytes 1859336 | tf_op jit(solution)/shard_map/ppermute | solution.py:20
  1507.1 43.8 %copy-start.103 = (bf16[1076,288]{0,1:T(8,128)(2,1)S(1)}, bf16[1076,288]{0,1:T(8,128)(2,1)}, u32[]{:S(2)}) copy-start(bf16[1076,288]{0,1:T(8,128)(2,1)} %reduce-scatter.11.cloned.1.call-done) | copy-start | bytes 1859332
  (149 other events, 532.6 us)
Sparse Core Ops, SparseCore 0:
  27.3 47.6 all-reduce.17
  94.1 44.9 all-reduce.19
  201.9 46.4 all-reduce.21
  284.2 72.6 all-reduce.37
  445.2 73.7 all-reduce.35
  606.2 71.8 all-reduce.33
  777.1 73.7 all-reduce.31
  912.2 44.1 all-reduce.23
  998.5 44.9 all-reduce.25
  1103.1 44.0 all-reduce.27
  1191.9 43.1 reduce-scatter.12
  1237.2 23.8 reduce-scatter.14
  1264.0 65.8 reduce-scatter.8
  1332.8 72.1 all-reduce.29
  1407.8 52.7 reduce-scatter.10
  1462.0 79.3 all-gather.2
  1542.9 53.4 all-gather.4
